TPU v7x, 32 devices: a whole 2x2x4 slice. The times are simulated.
32 devices in a mesh: region: 4 (over y, core), sub: 8 (over z, x).
Axes of the slice: x: 2, y: 2, z: 4, core: 2. Of those that a mesh axis runs over, the one named last changes fastest.
Arguments:
- coords: float32 [3, 2048, 128], P(None, ('region', 'sub')), may hold values from -3 to 3
- smooth: float32 [2048, 128], P(('region', 'sub')), may hold values from 0.6 to 1.5
- masses: float32 [2048, 128], P(('region', 'sub')), may hold values from 0.01 to 0.1
- owners: int32 [2048], P(('region', 'sub')), may hold values from 0 to 3, as said below
- counts: int32 [2048], P(('region', 'sub')), may hold values from 32 to 128
- neighbours: int32 [2048, 4], P(('region', 'sub')), may hold values from 0 to 71, as said below
Outputs:
- density: float32 [2048, 128], P(('region', 'sub'))
- accel: float32 [3, 2048, 128], P(None, ('region', 'sub'))
Inputs may be any that keep to these rules, and one draw needn't show every extreme that they name: `owners`: within the 64 tiles of each device's block, every value 0 to 4 - 1 appears exactly 16 times. `neighbours`: the first entry of the list of slot t is 4 + t (the tile itself); the entries of one list are distinct and lie within 4 of 4 + t.
All inputs are finite; a program needn't handle non-finite values.
Results may differ from a plain program's by a relative error of at most 0.0001.
Values sent between devices are 32-bit elements; how exact they have to be, the bound alone decides.
No kernel may reach another device: no remote copies, remote signals or barrier semaphores. Data moves between devices by JAX's collectives and lax.ppermute only.
A program may use at most 64 MiB of HBM per device.

v0:
```python
import math

import jax
import jax.numpy as jnp
from jax import lax
from jax.sharding import PartitionSpec as P

HALO_TILES = 4


kernel_scale = math.pi ** (-1.5)


def extended_2(x, sides, width):
    for axis, dim in sides:
        devices, length = (lax.axis_size(axis), x.shape[dim])
        up = [(i, (i + 1) % devices) for i in range(devices)]
        down = [(j, i) for i, j in up]
        last = lax.slice_in_dim(x, length - width, length, axis=dim)
        initial = lax.slice_in_dim(x, 0, width, axis=dim)
        before = lax.ppermute(last, axis, up)
        after = lax.ppermute(initial, axis, down)
        x = jnp.concatenate([before, x, after], axis=dim)
    return x


def pair_weights(pos_own, inverse_sq, kernel_norm, pos_partner):
    offset_vec = pos_own[:, :, :, None] - pos_partner[:, :, None, :]
    distance_sq = jnp.sum(offset_vec * offset_vec, axis=0)
    return (offset_vec, jnp.exp(-distance_sq * inverse_sq[:, :, None]) * kernel_norm[:, :, None])


def tile_terms(own_tiles):
    smooth_len = own_tiles[3]
    inverse_sq = 1.0 / (smooth_len * smooth_len)
    kernel_norm = kernel_scale * inverse_sq / smooth_len
    return (inverse_sq, kernel_norm)


def density_core(own_tiles, source, lists):
    inverse_sq, kernel_norm = tile_terms(own_tiles)
    partners = jnp.take(source, lists, axis=1)
    density = jnp.zeros(inverse_sq.shape, jnp.float32)
    for nb_slot in range(lists.shape[1]):
        partner = partners[:, :, nb_slot]
        unused, weight_pair = pair_weights(own_tiles[:3], inverse_sq, kernel_norm, partner[:3])
        density = density + jnp.sum(weight_pair * partner[4][:, None, :], axis=-1)
    return density


def force_pass(extended, pressure_ext, neighbours, pressure_own):
    tile_dev = neighbours.shape[0]
    own_tiles = extended[:, HALO_TILES : HALO_TILES + tile_dev]
    inverse_sq, kernel_norm = tile_terms(own_tiles)
    partners = jnp.take(extended, neighbours, axis=1)
    pressure_nb = jnp.take(pressure_ext, neighbours, axis=0)
    accel_sum = jnp.zeros((3,) + inverse_sq.shape, jnp.float32)
    for nb_slot in range(neighbours.shape[1]):
        partner = partners[:, :, nb_slot]
        offset_vec, weight_pair = pair_weights(own_tiles[:3], inverse_sq, kernel_norm, partner[:3])
        coefficient = (
            weight_pair
            * partner[4][:, None, :]
            * (pressure_own[:, :, None] + pressure_nb[:, nb_slot][:, None, :])
        )
        accel_sum = accel_sum + jnp.sum(offset_vec * coefficient[None], axis=-1)
    return 2.0 * inverse_sq[None] * accel_sum


def pressure_of(raw_density, live_mask):
    safe_density = jnp.where(live_mask > 0, raw_density, 1.0)
    return jnp.where(live_mask > 0, safe_density ** (-1.0 / 3.0), 0.0)


def per_device(coords, smooth, masses, owners, counts, neighbours):
    tile_dev, tile_rows = smooth.shape
    regions = lax.axis_size("region")
    per_dest = tile_dev // regions
    fields = jnp.concatenate([coords, smooth[None], masses[None]], axis=0)
    ordering = jnp.argsort(owners, stable=True)
    grouped = jnp.take(fields, ordering, axis=1).reshape(5, regions, per_dest, tile_rows)
    arrived = lax.all_to_all(grouped, "region", split_axis=1, concat_axis=1, tiled=True).reshape(
        5, tile_dev, tile_rows
    )
    slot_ids = jnp.arange(tile_rows, dtype=jnp.int32)
    live_mask = (slot_ids[None, :] < counts[:, None]).astype(jnp.float32)
    outgoing = jnp.concatenate([arrived[:4], (arrived[4] * live_mask)[None]], axis=0)
    extended = extended_2(outgoing, (("sub", 1),), HALO_TILES)
    own_tiles = extended[:, HALO_TILES : HALO_TILES + tile_dev]
    raw_density = density_core(own_tiles, extended, neighbours)
    pressure_own = pressure_of(raw_density, live_mask)
    pressure_ext = extended_2(pressure_own, (("sub", 0),), HALO_TILES)
    accel = force_pass(extended, pressure_ext, neighbours, pressure_own)
    return (raw_density * live_mask, accel * live_mask[None])


def solution(mesh):
    in_specs = (
        P(None, ("region", "sub"), None),
        P(("region", "sub"), None),
        P(("region", "sub"), None),
        P(("region", "sub")),
        P(("region", "sub")),
        P(("region", "sub"), None),
    )
    out_specs = (P(("region", "sub"), None), P(None, ("region", "sub"), None))
    return jax.shard_map(
        per_device, mesh=mesh, in_specs=in_specs, out_specs=out_specs, check_vma=False
    )
```

profile of v0, /device:TPU:0, one launch (start us, length us, event | category | flops | bytes accessed | tf_op | source)
XLA Modules:
  0.0 95.0 jit_solution(6657676319521581187)
XLA Ops:
  0.6 2.7 %sort.17 = (s32[64]{0:T(128)}, s32[64]{0:T(128)S(1)}) sort(s32[64]{0:T(128)} %param.11, s32[64]{0:T(128)S(1)} %iota.21), dimensions={0}, to_apply=%region_0.0 | sort | flops 384 | bytes 1024 | tf_op jit(solution)/shard_map/jit(argsort)/sort | solution.py:80
  3.3 1.0 %copy.43 = f32[3,64,128]{2,0,1:T(4,128)S(1)} copy(f32[3,64,128]{2,1,0:T(8,128)} %param.8) | data formatting | bytes 196608 | tf_op args[0]
  4.4 0.9 pad_maximum_fusion.1
  5.9 0.7 copy_select_fusion
  6.6 4.3 %all-to-all-start = ((f32[5,4,16,128]{3,2,0,1:T(8,128)}), f32[5,4,16,128]{3,2,0,1:T(8,128)S(1)}, u32[]{:S(2)}, u32[]{:S(2)}) async-start(f32[5,4,16,128]{3,2,0,1:T(8,128)} %copy_select_fusion), calls=%async_computation | async-start | bytes 327680 | tf_op jit(solution)/shard_map/all_to_all | solution.py:82
  10.9 0.7 compare_select_fusion.1
  11.6 0.7 fusion.12
  12.3 0.7 compare_and_fusion
  13.3 2.5 %all-to-all-done = f32[5,4,16,128]{3,2,0,1:T(8,128)S(1)} async-done(((f32[5,4,16,128]{3,2,0,1:T(8,128)}), f32[5,4,16,128]{3,2,0,1:T(8,128)S(1)}, u32[]{:S(2)}, u32[]{:S(2)}) %all-to-all-start) | async-done | bytes 163872 | tf_op jit(solution)/shard_map/all_to_all | solution.py:82
  15.9 0.8 compare_select_fusion
  16.8 5.1 %collective-permute-start.1 = (f32[5,4,128]{2,0,1:T(8,128)S(1)}, f32[5,4,128]{2,0,1:T(8,128)S(1)}, u32[]{:S(2)}, u32[]{:S(2)}) collective-permute-start(f32[5,4,128]{2,0,1:T(8,128)S(1)} %get-tuple-element.30), channel_id=1, source_target_pairs={{1,0},{2,1},{3,2},{4,3},{5,4},{6,5},{7,6},{0,7},{9,8},{10,9},{11,1... | collective-permute-start | bytes 30728 | tf_op jit(solution)/shard_map/ppermute | solution.py:22
  21.9 1.4 %collective-permute-done.1 = f32[5,4,128]{2,0,1:T(8,128)S(1)} collective-permute-done((f32[5,4,128]{2,0,1:T(8,128)S(1)}, f32[5,4,128]{2,0,1:T(8,128)S(1)}, u32[]{:S(2)}, u32[]{:S(2)}) %collective-permute-start.1) | collective-permute-done | bytes 10272 | tf_op jit(solution)/shard_map/ppermute | solution.py:22
  23.3 5.0 %collective-permute-done = f32[5,4,128]{2,0,1:T(8,128)S(1)} collective-permute-done((f32[5,4,128]{2,0,1:T(8,128)S(1)}, f32[5,4,128]{2,0,1:T(8,128)S(1)}, u32[]{:S(2)}, u32[]{:S(2)}) %collective-permute-start) | collective-permute-done | bytes 10272 | tf_op jit(solution)/shard_map/ppermute | solution.py:21
  28.4 1.0 %gather_fusion.2 = f32[256,5,128]{2,1,0:T(8,128)S(1)} fusion(f32[5,72,128]{2,0,1:T(8,128)S(1)} %pad_maximum_fusion, s32[1024]{0:T(1024)S(1)} %pad_clamp_fusion), kind=kCustom, calls=%fused_computation.clone | custom fusion | bytes 1311744 | tf_op jit(solution)/shard_map/jit(_take)/gather | solution.py:42
  30.1 16.2 %fusion.2 = (f32[64,128,128]{2,1,0:T(8,128)S(1)}, f32[64,128,128]{2,1,0:T(8,128)}, f32[64,128,128]{2,1,0:T(8,128)}, f32[64,128,128]{2,1,0:T(8,128)}) fusion(f32[3,64,128]{2,1,0:T(8,128)S(1)} %copy.50, f32[3,64,128]{2,1,0:T(8,128)S(1)} %bitcast.40, f32[3,64,128]{2,1,0:T(8,128)S(1)} %copy.51, f32[3,64,128]{2,1,0:T(8,128)S(1)} %copy.52, f32[3,64,128]{2,1,0:T(8,128)S(1)} %copy.49), kind=kLoop, calls=%fused_computation.13 | loop fusion | flops 33554432 | bytes 17268736 | tf_op jit(solution)/shard_map/reduce_sum | solution.py:29
  46.3 12.1 %fusion.9 = (f32[64,128]{1,0:T(8,128)S(1)}, f32[64,128]{1,0:T(8,128)S(1)}, f32[64,128]{1,0:T(8,128)S(1)}, f32[64,128]{1,0:T(8,128)S(1)}) fusion(f32[64,128,128]{2,1,0:T(8,128)S(1)} %get-tuple-element.9, f32[64,128]{1,0:T(8,128)S(1)} %bitcast.50, f32[64,128]{1,0:T(8,128)S(1)} %get-tuple-element.41, f32[64,128]{1,0:T(8,128)S(1)} %get-tuple-element.40, ...), kind=kLoop, calls=%fused_computation.28 | loop fusion | flops 20938752 | bytes 17104896 | tf_op jit(solution)/shard_map/reduce_sum | solution.py:47
  58.5 2.0 %collective-permute-start.2 = (f32[4,128]{1,0:T(4,128)S(1)}, f32[4,128]{1,0:T(4,128)S(1)}, u32[]{:S(2)}, u32[]{:S(2)}) collective-permute-start(f32[4,128]{1,0:T(4,128)S(1)} %get-tuple-element.42), channel_id=1, source_target_pairs={{0,1},{1,2},{2,3},{3,4},{4,5},{5,6},{6,7},{7,0},{8,9},{9,10},{10,1... | collective-permute-start | bytes 6152 | tf_op jit(solution)/shard_map/ppermute | solution.py:21
  60.6 0.7 fusion.13
  61.2 0.9 collective-permute-done.3
  62.1 2.8 %collective-permute-done.2 = f32[4,128]{1,0:T(4,128)S(1)} collective-permute-done((f32[4,128]{1,0:T(4,128)S(1)}, f32[4,128]{1,0:T(4,128)S(1)}, u32[]{:S(2)}, u32[]{:S(2)}) %collective-permute-start.2) | collective-permute-done | bytes 2080 | tf_op jit(solution)/shard_map/ppermute | solution.py:21
  64.9 0.7 gather_fusion.1
  65.9 7.9 %add_multiply_fusion.3 = (f32[64,128,128]{2,1,0:T(8,128)S(1)}, f32[64,128,128]{2,1,0:T(8,128)S(1)}, f32[64,128,128]{2,1,0:T(8,128)S(1)}, f32[64,128,128]{2,1,0:T(8,128)S(1)}) fusion(f32[64,128,128]{2,1,0:T(8,128)} %get-tuple-element.12, f32[64,128]{1,0:T(8,128)S(1)} %bitcast.52, f32[64,128]{1,0:T(8,128)S(1)} %get-tuple-element.17, ...), kind=kLoop, calls=%fused_computation.22 | loop fusion | flops 25165824 | bytes 33914880 | tf_op jit(solution)/shard_map/mul | solution.py:62
  73.7 20.6 %fusion.3 = (f32[3,64,128]{2,1,0:T(8,128)S(1)}, f32[3,64,128]{2,1,0:T(8,128)S(1)}, f32[3,64,128]{2,1,0:T(8,128)S(1)}, f32[3,64,128]{2,1,0:T(8,128)S(1)}) fusion(f32[64,128,128]{2,1,0:T(8,128)S(1)} %get-tuple-element.36, f32[3,64,128]{2,1,0:T(8,128)S(1)} %copy.50, f32[3,64,128]{2,1,0:T(8,128)S(1)} %bitcast.41, f32[64,128,128]{2,1,0:T(8,128)S(1)} %get-tuple-element.38, ...), kind=kLoop, calls=%fused_computation.14 | loop fusion | flops 37650432 | bytes 17661952 | tf_op jit(solution)/shard_map/reduce_sum | solution.py:66
  94.3 0.7 multiply_multiply_fusion.4
  (36 shorter events, 2.3 us)
Async XLA Ops:
  6.6 9.2 %all-to-all-start = ((f32[5,4,16,128]{3,2,0,1:T(8,128)}), f32[5,4,16,128]{3,2,0,1:T(8,128)S(1)}, u32[]{:S(2)}, u32[]{:S(2)}) async-start(f32[5,4,16,128]{3,2,0,1:T(8,128)} %copy_select_fusion), calls=%async_computation | async-start | bytes 327680 | tf_op jit(solution)/shard_map/all_to_all | solution.py:82
  16.8 6.6 %collective-permute-start.1 = (f32[5,4,128]{2,0,1:T(8,128)S(1)}, f32[5,4,128]{2,0,1:T(8,128)S(1)}, u32[]{:S(2)}, u32[]{:S(2)}) collective-permute-start(f32[5,4,128]{2,0,1:T(8,128)S(1)} %get-tuple-element.30), channel_id=1, source_target_pairs={{1,0},{2,1},{3,2},{4,3},{5,4},{6,5},{7,6},{0,7},{9,8},{10,9},{11,1... | collective-permute-start | bytes 30728 | tf_op jit(solution)/shard_map/ppermute | solution.py:22
  21.9 6.4 %collective-permute-start = (f32[5,4,128]{2,0,1:T(8,128)S(1)}, f32[5,4,128]{2,0,1:T(8,128)S(1)}, u32[]{:S(2)}, u32[]{:S(2)}) collective-permute-start(f32[5,4,128]{2,0,1:T(8,128)S(1)} %get-tuple-element.29), channel_id=1, source_target_pairs={{0,1},{1,2},{2,3},{3,4},{4,5},{5,6},{6,7},{7,0},{8,9},{9,10},{10,1... | collective-permute-start | bytes 30728 | tf_op jit(solution)/shard_map/ppermute | solution.py:21
  46.3 12.1 %copy-start = (f32[64,128,128]{2,1,0:T(8,128)}, f32[64,128,128]{2,1,0:T(8,128)S(1)}, u32[]{:S(2)}) copy-start(f32[64,128,128]{2,1,0:T(8,128)S(1)} %get-tuple-element.9) | copy-start | bytes 12582916
  46.3 12.1 %copy-start.1 = (s32[64]{0:T(128)S(1)}, s32[64]{0:T(128)}, u32[]{:S(2)}) copy-start(s32[64]{0:T(128)} %param.12) | copy-start | bytes 772
  58.5 3.6 %collective-permute-start.3 = (f32[4,128]{1,0:T(4,128)S(1)}, f32[4,128]{1,0:T(4,128)S(1)}, u32[]{:S(2)}, u32[]{:S(2)}) collective-permute-start(f32[4,128]{1,0:T(4,128)S(1)} %get-tuple-element.43), channel_id=1, source_target_pairs={{1,0},{2,1},{3,2},{4,3},{5,4},{6,5},{7,6},{0,7},{9,8},{10,9},{11,1... | collective-permute-start | bytes 6152 | tf_op jit(solution)/shard_map/ppermute | solution.py:22
  58.5 6.3 %collective-permute-start.2 = (f32[4,128]{1,0:T(4,128)S(1)}, f32[4,128]{1,0:T(4,128)S(1)}, u32[]{:S(2)}, u32[]{:S(2)}) collective-permute-start(f32[4,128]{1,0:T(4,128)S(1)} %get-tuple-element.42), channel_id=1, source_target_pairs={{0,1},{1,2},{2,3},{3,4},{4,5},{5,6},{6,7},{7,0},{8,9},{9,10},{10,1... | collective-permute-start | bytes 6152 | tf_op jit(solution)/shard_map/ppermute | solution.py:21
where the time goes:
time: 95.4 us; the launch traced here: 95 us
  other arithmetic  65.9 us (69%)
  waiting for transfers between devices  12.5 us (13%)
  starting transfers between devices  11.4 us (12%)
  local copies, waits for them, and re-layouts  4.21 us (4%)
    reduce_sum x1, other arithmetic, force_pass(): accel_sum = accel_sum + jnp.sum(offset_vec * coefficient[None], axis=-1)  20.6 us
    reduce_sum x1, other arithmetic, pair_weights(): distance_sq = jnp.sum(offset_vec * offset_vec, axis=0)  16.2 us
    reduce_sum x1, other arithmetic, density_core(): density = density + jnp.sum(weight_pair * partner[4][:, None, :], axis=-1)  12.1 us
    mul x1, other arithmetic, force_pass(): weight_pair * partner[4][:, None, :]  7.85 us
    ppermute x2, waiting for transfers between devices, extended_2(): before = lax.ppermute(last, axis, up)  7.75 us
    ppermute x2, starting transfers between devices, extended_2(): after = lax.ppermute(initial, axis, down)  5.17 us
    all_to_all x1, starting transfers between devices, per_device(): lax.all_to_all(grouped, 'region', split_axis=1, concat_axis=1, tiled=True)  4.26 us
    sort x1, other arithmetic, per_device(): ordering = jnp.argsort(owners, stable=True)  2.69 us
  transfers between devices with their start and end apart: 5, of which 5 were waited for; matrix products, arithmetic and copies ran while one was open for 3% of the time, Pallas kernels for 0%

commit v1 on v0

v1 whole, which is shorter than its diff:
```python
import functools
import math

import jax
import jax.numpy as jnp
from jax import lax
from jax.experimental import pallas as pl
from jax.experimental.pallas import tpu as pltpu
from jax.sharding import PartitionSpec as P

HALO_TILES = 4
RIM = 2 * HALO_TILES
FIELDS = 5
FEATURES = 32
SUMS = 16
EMPTY_LOG = -1024.0
LOG2E = 1.4426950408889634
kernel_scale = math.pi ** (-1.5)

f32, bf16 = jnp.float32, jnp.bfloat16
VMEM = pl.BlockSpec(memory_space=pltpu.VMEM)
SMEM = pl.BlockSpec(memory_space=pltpu.SMEM)


def group_kernel(per_dest, owners_ref, coords_ref, smooth_ref, masses_ref, out_ref, seen_ref):
    regions = out_ref.shape[0]
    for d in range(regions):
        seen_ref[d] = 0

    @pl.loop(0, owners_ref.shape[0], unroll=8)
    def _(n):
        d = owners_ref[n]
        k = seen_ref[d]
        seen_ref[d] = k + 1
        for c in range(3):
            out_ref[d, pl.ds(c * per_dest + k, 1)] = coords_ref[c, pl.ds(n, 1)]
        out_ref[d, pl.ds(3 * per_dest + k, 1)] = smooth_ref[pl.ds(n, 1)]
        out_ref[d, pl.ds(4 * per_dest + k, 1)] = masses_ref[pl.ds(n, 1)]


def group_tiles(coords, smooth, masses, owners, regions):
    tile_dev, rows = smooth.shape
    per_dest = tile_dev // regions
    return pl.pallas_call(
        functools.partial(group_kernel, per_dest),
        out_shape=jax.ShapeDtypeStruct((regions, FIELDS * per_dest, rows), f32),
        in_specs=[SMEM, VMEM, VMEM, VMEM],
        out_specs=VMEM,
        scratch_shapes=[pltpu.SMEM((regions,), jnp.int32)],
        name="group_tiles",
    )(owners, coords, smooth, masses)


def parts_of(x, count):
    parts = []
    for i in range(count):
        part = x.astype(bf16).astype(f32)
        parts.append(part)
        x = x - part
    return parts


def dot(a, b):
    return jnp.dot(a, b, preferred_element_type=f32)


def sph_kernel(
    tile_dev, unroll, lists_ref, rim_lists_ref, own_ref, live_ref, below_ref, above_ref, density_ref, accel_ref,
    feat_ref, featT_ref, own_feat_ref, coef_ref, coefb_ref, high_ref, low_ref, sum_ref, out_ref, q_ref,
):
    rows = own_ref.shape[-1]
    ext = tile_dev + 2 * RIM
    regions, per_dest = own_ref.shape[0], tile_dev // own_ref.shape[0]

    def field(f):
        own = jnp.concatenate([own_ref[r, f * per_dest:(f + 1) * per_dest] for r in range(regions)], axis=0)
        if f == 4:
            own = own * live_ref[...]
        return jnp.concatenate([below_ref[f * RIM:(f + 1) * RIM], own, above_ref[f * RIM:(f + 1) * RIM]], axis=0)

    pos = [field(f) for f in range(3)]
    h = field(3)
    mass = field(4)
    live = mass > 0
    inverse_sq = 1.0 / (h * h)
    norm = kernel_scale * inverse_sq / h
    c = inverse_sq * LOG2E
    square = pos[0] * pos[0] + pos[1] * pos[1] + pos[2] * pos[2]
    log_mass = jnp.where(live, jnp.log2(jnp.where(live, mass, 1.0)), EMPTY_LOG)
    one, zero = jnp.ones_like(c), jnp.zeros_like(c)
    partner_rows, own_rows = [], []
    for value, own in [(pos[0], 2 * c * pos[0]), (pos[1], 2 * c * pos[1]), (pos[2], 2 * c * pos[2]), (square, -c)]:
        p1, p2, p3 = parts_of(value, 3)
        o1, o2, o3 = parts_of(own, 3)
        partner_rows += [p1, p1, p2, p1, p3, p2]
        own_rows += [o1, o2, o1, o3, o1, o2]
    partner_rows += parts_of(log_mass, 3) + [one] * 3 + [zero] * 2
    own_rows += [one] * 3 + parts_of(-c * square, 3) + [zero] * 2
    for k in range(FEATURES):
        feat_ref[:, k] = partner_rows[k]

    def turn(e):
        block = feat_ref[e]
        featT_ref[e] = jnp.concatenate([block, block], axis=0).T.astype(bf16)

    pl.loop(0, ext, unroll=4)(turn)
    for k in range(FEATURES):
        feat_ref[:, k] = own_rows[k]
    blank = jnp.zeros((FEATURES, rows), f32)

    def pair_up(p):
        e = HALO_TILES + 2 * p
        a, b = feat_ref[e], feat_ref[e + 1]
        top = jnp.concatenate([a, blank], axis=1)
        low = jnp.concatenate([blank, b], axis=1)
        own_feat_ref[p] = jnp.concatenate([top, low], axis=0).astype(bf16)

    pairs = (tile_dev + RIM) // 2
    pl.loop(0, pairs, unroll=4)(pair_up)

    lane = lax.broadcasted_iota(jnp.int32, (rows, 2 * FEATURES), 1)
    first_half = lane < FEATURES

    def weights(p, partners):
        own = own_feat_ref[p]
        for e0, e1 in partners:
            left = jnp.where(first_half, featT_ref[e0], featT_ref[e1])
            yield jnp.exp2(dot(left, own))

    def density_pair(p, partners, store_at):
        total = None
        for n, t in enumerate(weights(p, partners)):
            if store_at is not None:
                high = t.astype(bf16)
                high_ref[store_at, n * rows:(n + 1) * rows] = high
                low_ref[store_at, n * rows:(n + 1) * rows] = (t - high.astype(f32)).astype(bf16)
            part = jnp.sum(t.reshape(rows // 8, 8, 2 * rows), axis=0)
            total = part if total is None else total + part
        total = jnp.sum(total, axis=0, keepdims=True)
        sum_ref[pl.ds(2 * p, 1)] = total[:, :rows]
        sum_ref[pl.ds(2 * p + 1, 1)] = total[:, rows:]

    listed = lists_ref.shape[1]

    def own_partners(u):
        return [(lists_ref[2 * u, n] + HALO_TILES, lists_ref[2 * u + 1, n] + HALO_TILES) for n in range(listed)]

    rim_pairs = HALO_TILES // 2
    for u in range(2 * rim_pairs):
        shift = HALO_TILES - tile_dev if u < rim_pairs else HALO_TILES + tile_dev
        partners = [
            (rim_lists_ref[2 * u * listed + n] + shift, rim_lists_ref[(2 * u + 1) * listed + n] + shift)
            for n in range(listed)
        ]
        density_pair(u if u < rim_pairs else u + tile_dev // 2, partners, None)

    @pl.loop(0, tile_dev // 2, unroll=unroll)
    def _(u):
        density_pair(u + rim_pairs, own_partners(u), u)

    inner = slice(HALO_TILES, ext - HALO_TILES)
    raw = sum_ref[...] * norm[inner]
    inner_live = live[inner]
    q = jnp.where(inner_live, jnp.exp2(jnp.log2(jnp.where(inner_live, raw, 1.0)) * (-1.0 / 3.0)), 0.0)
    pad = jnp.zeros((HALO_TILES, rows), f32)
    q = jnp.concatenate([pad, q, pad], axis=0)
    coef = [one]
    for value in pos + [q] + [q * x for x in pos]:
        coef += parts_of(value, 2)
    coef.append(zero)
    for k in range(SUMS):
        coef_ref[:, k] = coef[k]

    def narrow(e):
        coefb_ref[e] = coef_ref[e].astype(bf16)

    pl.loop(0, ext, unroll=8)(narrow)

    @pl.loop(0, tile_dev // 2, unroll=unroll)
    def _(u):
        total = None
        for n, (e0, e1) in enumerate(own_partners(u)):
            left = jnp.concatenate([coefb_ref[e0], coefb_ref[e1]], axis=0)
            part = dot(left, high_ref[u, n * rows:(n + 1) * rows]) + dot(left, low_ref[u, n * rows:(n + 1) * rows])
            total = part if total is None else total + part
        out_ref[2 * u] = total[:SUMS, :rows]
        out_ref[2 * u + 1] = total[SUMS:, rows:]

    mine = slice(RIM, RIM + tile_dev)
    own_live = live_ref[...]
    density_ref[...] = raw[HALO_TILES:HALO_TILES + tile_dev] * own_live
    q_own = q[mine]
    scale = own_live * (2.0 * inverse_sq[mine] * norm[mine])
    s0 = out_ref[:, 0]
    q0 = out_ref[:, 7] + out_ref[:, 8]
    for c in range(3):
        s1 = out_ref[:, 1 + 2 * c] + out_ref[:, 2 + 2 * c]
        q1 = out_ref[:, 9 + 2 * c] + out_ref[:, 10 + 2 * c]
        x = pos[c][mine]
        accel_ref[c] = scale * (q_own * (x * s0 - s1) + (x * q0 - q1))


def sph(lists, rim_lists, own, live, below, above):
    tile_dev, rows = live.shape
    ext = tile_dev + 2 * RIM
    listed = lists.shape[1]
    pairs = (tile_dev + RIM) // 2
    return pl.pallas_call(
        functools.partial(sph_kernel, tile_dev, 4),
        out_shape=(jax.ShapeDtypeStruct((tile_dev, rows), f32), jax.ShapeDtypeStruct((3, tile_dev, rows), f32)),
        in_specs=[SMEM, SMEM, VMEM, VMEM, VMEM, VMEM],
        out_specs=(VMEM, VMEM),
        scratch_shapes=[
            pltpu.VMEM((ext, FEATURES, rows), f32),
            pltpu.VMEM((ext, rows, 2 * FEATURES), bf16),
            pltpu.VMEM((pairs, 2 * FEATURES, 2 * rows), bf16),
            pltpu.VMEM((ext, SUMS, rows), f32),
            pltpu.VMEM((ext, SUMS, rows), bf16),
            pltpu.VMEM((tile_dev // 2, listed * rows, 2 * rows), bf16),
            pltpu.VMEM((tile_dev // 2, listed * rows, 2 * rows), bf16),
            pltpu.VMEM((tile_dev + RIM, rows), f32),
            pltpu.VMEM((tile_dev, SUMS, rows), f32),
            pltpu.VMEM((8, rows), f32),
        ],
        name="sph",
    )(lists, rim_lists, own, live, below, above)


def per_device(coords, smooth, masses, owners, counts, neighbours):
    tile_dev, rows = smooth.shape
    regions = lax.axis_size("region")
    subs = lax.axis_size("sub")
    per_dest = tile_dev // regions
    listed = neighbours.shape[1]
    grouped = group_tiles(coords, smooth, masses, owners, regions)
    own = lax.all_to_all(grouped, "region", 0, 0, tiled=True)
    live = (jnp.arange(rows, dtype=jnp.int32)[None, :] < counts[:, None]).astype(f32)
    by_field = own.reshape(regions, FIELDS, per_dest, rows)

    def rim(first):
        if per_dest >= RIM:
            block = by_field[regions - 1 if not first else 0]
            block = block[:, :RIM] if first else block[:, per_dest - RIM:]
        else:
            blocks = RIM // per_dest
            block = by_field[:blocks] if first else by_field[regions - blocks:]
            block = jnp.swapaxes(block, 0, 1).reshape(FIELDS, RIM, rows)
        tiles = slice(0, RIM) if first else slice(tile_dev - RIM, tile_dev)
        block = jnp.concatenate([block[:4], (block[4] * live[tiles])[None]], axis=0).reshape(FIELDS * RIM, rows)
        near = slice(0, HALO_TILES) if first else slice(tile_dev - HALO_TILES, tile_dev)
        ids = neighbours[near].astype(f32).reshape(1, HALO_TILES * listed)
        return jnp.concatenate([block, jnp.pad(ids, ((0, 7), (0, rows - HALO_TILES * listed)))], axis=0)

    up = [(i, (i + 1) % subs) for i in range(subs)]
    down = [(j, i) for i, j in up]
    below = lax.ppermute(rim(False), "sub", up)
    above = lax.ppermute(rim(True), "sub", down)
    count = HALO_TILES * listed
    rim_lists = jnp.concatenate([below[FIELDS * RIM, :count], above[FIELDS * RIM, :count]]).astype(jnp.int32)
    return sph(neighbours, rim_lists, own, live, below, above)


def solution(mesh):
    in_specs = (
        P(None, ("region", "sub"), None),
        P(("region", "sub"), None),
        P(("region", "sub"), None),
        P(("region", "sub")),
        P(("region", "sub")),
        P(("region", "sub"), None),
    )
    out_specs = (P(("region", "sub"), None), P(None, ("region", "sub"), None))
    return jax.shard_map(
        per_device, mesh=mesh, in_specs=in_specs, out_specs=out_specs, check_vma=False
    )
```

time: 95.4 us -> 41.1 us (0.43)
  other arithmetic: 65.9 us -> 0.79 us
  Pallas kernels: 0 us -> 17.9 us
  waiting for transfers between devices: 12.5 us -> 9.67 us
  local copies, waits for them, and re-layouts: 4.21 us -> 2.24 us
  starting transfers between devices: 11.4 us -> 9.51 us
    reduce_sum x3 -> x0, other arithmetic: 48.8 us -> none  [the longest x1 20.6 us: force_pass(): accel_sum = accel_sum + jnp.sum(offset_vec * coefficient[None], axis=-1)]
    pallas_call x0 -> x2, Pallas kernels: none -> 17.9 us  [the longest x1 16 us: sph(): pl.pallas_call(functools.partial(sph_kernel, tile_dev, 4), out_shape=(jax...]
    mul x5 -> x0, other arithmetic: 10 us -> none  [the longest x1 7.85 us: force_pass(): weight_pair * partner[4][:, None, :]]
    ppermute x4 -> x2, waiting for transfers between devices: 10 us -> 6.51 us  [the longest x1 5.06 us: per_device(): below = lax.ppermute(rim(False), 'sub', up)]
    sort x1 -> x0, other arithmetic: 2.69 us -> none  [per_device(): ordering = jnp.argsort(owners, stable=True)]
    gather x3 -> x0, local copies, waits for them, and re-layouts: 2.39 us -> none  [the longest x1 1.03 us: density_core(): partners = jnp.take(source, lists, axis=1)]
    ppermute x4 -> x2, starting transfers between devices: 7.18 us -> 5.12 us  [the longest x1 5.06 us: per_device(): above = lax.ppermute(rim(True), 'sub', down)]
    select_n x6 -> x0, other arithmetic: 2.02 us -> none  [the longest x2 1.02 us: density_core(): partners = jnp.take(source, lists, axis=1)]
  transfers between devices with their start and end apart: 5 -> 3, of which waited for: 5 -> 3; matrix products, arithmetic and copies ran while one was open for 3% -> 3% of each run, Pallas kernels for 0% -> 0%
where the time goes in v1:
time: 41.1 us; the launch traced here: 40.8 us
  Pallas kernels  17.9 us (44%)
  waiting for transfers between devices  9.67 us (24%)
  starting transfers between devices  9.51 us (23%)
  local copies, waits for them, and re-layouts  2.24 us (5%)
  other arithmetic  0.79 us (2%)
  between operations  0.71 us (2%)
    pallas_call x1, Pallas kernels, sph(): pl.pallas_call(functools.partial(sph_kernel, tile_dev, 4), out_shape=(jax...  16 us
    ppermute x1, waiting for transfers between devices, per_device(): below = lax.ppermute(rim(False), 'sub', up)  5.06 us
    ppermute x1, starting transfers between devices, per_device(): above = lax.ppermute(rim(True), 'sub', down)  5.06 us
    all_to_all x1, starting transfers between devices, per_device(): own = lax.all_to_all(grouped, 'region', 0, 0, tiled=True)  4.4 us
    all_to_all x1, waiting for transfers between devices, per_device(): own = lax.all_to_all(grouped, 'region', 0, 0, tiled=True)  3.17 us
    pallas_call x1, Pallas kernels, group_tiles(): pl.pallas_call(functools.partial(group_kernel, per_dest), out_shape=jax.S...  1.9 us
    unnamed x13, local copies, waits for them, and re-layouts  1.87 us
    ppermute x1, waiting for transfers between devices, per_device(): above = lax.ppermute(rim(True), 'sub', down)  1.44 us
  transfers between devices with their start and end apart: 3, of which 3 were waited for; matrix products, arithmetic and copies ran while one was open for 3% of the time, Pallas kernels for 0%

profile of v1, /device:TPU:0, one launch (start us, length us, event | category | flops | bytes accessed | tf_op | source)
XLA Modules:
  0.0 40.8 jit_solution(9484141917071713270)
XLA Ops:
  0.6 1.9 %group_tiles.1 = f32[4,80,128]{2,1,0:T(8,128)} custom-call(s32[64]{0:T(128)} %owners_ref.1, f32[3,64,128]{2,1,0:T(8,128)} %coords_ref.1, f32[64,128]{1,0:T(8,128)} %smooth_ref.1, f32[64,128]{1,0:T(8,128)} %masses_ref.1), custom_call_target="tpu_custom_call" | custom-call | tf_op jit(solution)/shard_map/group_tiles/pallas_call | solution.py:44
  2.5 4.4 %all-to-all-start = ((f32[4,80,128]{2,1,0:T(8,128)}), f32[4,80,128]{2,1,0:T(8,128)S(1)}, u32[]{:S(2)}, u32[]{:S(2)}) async-start(f32[4,80,128]{2,1,0:T(8,128)} %group_tiles.1), calls=%async_computation | async-start | bytes 327680 | tf_op jit(solution)/shard_map/all_to_all | solution.py:236
  6.9 0.0 copy-done.4
  6.9 0.1 slice_convert_fusion.1
  7.0 0.7 %copy.10.lists_ref = s32[64,4]{1,0:T(8,128)} copy(s32[64,4]{0,1:T(4,128)S(1)} %copy-done.4) | data formatting | bytes 2048 | tf_op args[5]
  7.7 0.1 copy.8
  7.8 0.1 reshape.23
  7.9 0.1 copy.9
  8.0 0.0 copy-start.5
  8.0 0.1 reshape.25
  8.1 0.6 %copy-done.5 = s32[64]{0:T(128)S(1)} copy-done((s32[64]{0:T(128)S(1)}, s32[64]{0:T(128)}, u32[]{:S(2)}) %copy-start.5) | copy-done | bytes 280
  8.6 0.1 fusion.live_ref
  8.7 0.0 copy-start.1
  8.7 3.2 %all-to-all-done.own_ref = f32[4,80,128]{2,1,0:T(8,128)S(1)} async-done(((f32[4,80,128]{2,1,0:T(8,128)}), f32[4,80,128]{2,1,0:T(8,128)S(1)}, u32[]{:S(2)}, u32[]{:S(2)}) %all-to-all-start) | async-done | bytes 163872 | tf_op jit(solution)/shard_map/all_to_all | solution.py:236
  11.9 0.0 copy-done.1
  12.0 0.6 %copy-done = f32[4,80,128]{2,1,0:T(8,128)} copy-done((f32[4,80,128]{2,1,0:T(8,128)}, f32[4,80,128]{2,1,0:T(8,128)S(1)}, u32[]{:S(2)}) %copy-start) | copy-done | bytes 163864
  12.6 5.1 %collective-permute-start.1 = (f32[48,128]{1,0:T(8,128)S(1)}, f32[48,128]{1,0:T(8,128)S(1)}, u32[]{:S(2)}, u32[]{:S(2)}) collective-permute-start(f32[48,128]{1,0:T(8,128)S(1)} %select_maximum_fusion), channel_id=1, source_target_pairs={{1,0},{2,1},{3,2},{4,3},{5,4},{6,5},{7,6},{0,7},{9,8},{10,9},{11,1... | collective-permute-start | bytes 73736 | tf_op jit(solution)/shard_map/ppermute | solution.py:257
  17.6 0.1 collective-permute-start
  17.7 1.4 %collective-permute-done.1.above_ref = f32[48,128]{1,0:T(8,128)S(1)} collective-permute-done((f32[48,128]{1,0:T(8,128)S(1)}, f32[48,128]{1,0:T(8,128)S(1)}, u32[]{:S(2)}, u32[]{:S(2)}) %collective-permute-start.1) | collective-permute-done | bytes 24608 | tf_op jit(solution)/shard_map/ppermute | solution.py:257
  19.1 5.1 %collective-permute-done.below_ref = f32[48,128]{1,0:T(8,128)S(1)} collective-permute-done((f32[48,128]{1,0:T(8,128)S(1)}, f32[48,128]{1,0:T(8,128)S(1)}, u32[]{:S(2)}, u32[]{:S(2)}) %collective-permute-start) | collective-permute-done | bytes 24608 | tf_op jit(solution)/shard_map/ppermute | solution.py:256
  24.2 0.6 %maximum_convert_fusion.rim_lists_ref = s32[32]{0:T(128)} fusion(f32[16]{0:T(128)S(1)} %slice_bitcast_fusion.2, f32[16]{0:T(128)S(1)} %slice_bitcast_fusion.3), kind=kLoop, calls=%fused_computation.17 | loop fusion | flops 64 | bytes 256 | tf_op jit(solution)/shard_map/convert_element_type | solution.py:259
  24.8 0.0 copy-done.2
  24.8 0.0 copy-done.3
  24.8 16.0 %sph.1 = (f32[64,128]{1,0:T(8,128)}, f32[3,64,128]{2,1,0:T(8,128)}) custom-call(s32[64,4]{1,0:T(8,128)} %copy.10.lists_ref, s32[32]{0:T(128)} %maximum_convert_fusion.rim_lists_ref, f32[4,80,128]{2,1,0:T(8,128)} %copy-done, f32[64,128]{1,0:T(8,128)} %copy-done.1, f32[48,128]{1,0:T(8,128)} %copy-done.3, f32[48,128]{1,0:T(8,128)} %copy-done.2), custom_call_target="tpu_custom_call" | custom-call | tf_op jit(solution)/shard_map/sph/pallas_call | solution.py:208
  (14 shorter events, 0.1 us)
Async XLA Ops:
  2.5 4.4 %copy-start.4 = (s32[64,4]{0,1:T(4,128)S(1)}, s32[64,4]{0,1:T(4,128)}, u32[]{:S(2)}) copy-start(s32[64,4]{0,1:T(4,128)} %param.11) | copy-start | bytes 3076
  2.5 9.3 %all-to-all-start = ((f32[4,80,128]{2,1,0:T(8,128)}), f32[4,80,128]{2,1,0:T(8,128)S(1)}, u32[]{:S(2)}, u32[]{:S(2)}) async-start(f32[4,80,128]{2,1,0:T(8,128)} %group_tiles.1), calls=%async_computation | async-start | bytes 327680 | tf_op jit(solution)/shard_map/all_to_all | solution.py:236
  8.0 0.7 %copy-start.5 = (s32[64]{0:T(128)S(1)}, s32[64]{0:T(128)}, u32[]{:S(2)}) copy-start(s32[64]{0:T(128)} %param.10) | copy-start | bytes 772
  8.7 3.2 %copy-start.1 = (f32[64,128]{1,0:T(8,128)}, f32[64,128]{1,0:T(8,128)S(1)}, u32[]{:S(2)}) copy-start(f32[64,128]{1,0:T(8,128)S(1)} %fusion.live_ref) | copy-start | bytes 98308
  11.9 0.7 %copy-start = (f32[4,80,128]{2,1,0:T(8,128)}, f32[4,80,128]{2,1,0:T(8,128)S(1)}, u32[]{:S(2)}) copy-start(f32[4,80,128]{2,1,0:T(8,128)S(1)} %all-to-all-done.own_ref) | copy-start | bytes 491524
  12.6 6.6 %collective-permute-start.1 = (f32[48,128]{1,0:T(8,128)S(1)}, f32[48,128]{1,0:T(8,128)S(1)}, u32[]{:S(2)}, u32[]{:S(2)}) collective-permute-start(f32[48,128]{1,0:T(8,128)S(1)} %select_maximum_fusion), channel_id=1, source_target_pairs={{1,0},{2,1},{3,2},{4,3},{5,4},{6,5},{7,6},{0,7},{9,8},{10,9},{11,1... | collective-permute-start | bytes 73736 | tf_op jit(solution)/shard_map/ppermute | solution.py:257
  17.6 6.6 %collective-permute-start = (f32[48,128]{1,0:T(8,128)S(1)}, f32[48,128]{1,0:T(8,128)S(1)}, u32[]{:S(2)}, u32[]{:S(2)}) collective-permute-start(f32[48,128]{1,0:T(8,128)S(1)} %select_maximum_fusion.1), channel_id=1, source_target_pairs={{0,1},{1,2},{2,3},{3,4},{4,5},{5,6},{6,7},{7,0},{8,9},{9,10},{10,1... | collective-permute-start | bytes 73736 | tf_op jit(solution)/shard_map/ppermute | solution.py:256
  19.1 5.7 %copy-start.2 = (f32[48,128]{1,0:T(8,128)}, f32[48,128]{1,0:T(8,128)S(1)}, u32[]{:S(2)}) copy-start(f32[48,128]{1,0:T(8,128)S(1)} %collective-permute-done.1.above_ref) | copy-start | bytes 73732
  24.2 0.6 %copy-start.3 = (f32[48,128]{1,0:T(8,128)}, f32[48,128]{1,0:T(8,128)S(1)}, u32[]{:S(2)}) copy-start(f32[48,128]{1,0:T(8,128)S(1)} %collective-permute-done.below_ref) | copy-start | bytes 73732

commit v2 on v1

--- a/solution.py
+++ b/solution.py
@@ -8,11 +8,11 @@
 from jax.experimental.pallas import tpu as pltpu
 from jax.sharding import PartitionSpec as P
 
+
 HALO_TILES = 4
 RIM = 2 * HALO_TILES
 FIELDS = 5
-FEATURES = 32
-SUMS = 16
+DEPTH = 48
 EMPTY_LOG = -1024.0
 LOG2E = 1.4426950408889634
 kernel_scale = math.pi ** (-1.5)
@@ -47,13 +47,14 @@
         in_specs=[SMEM, VMEM, VMEM, VMEM],
         out_specs=VMEM,
         scratch_shapes=[pltpu.SMEM((regions,), jnp.int32)],
+        compiler_params=pltpu.CompilerParams(vmem_limit_bytes=8 << 20),
         name="group_tiles",
     )(owners, coords, smooth, masses)
 
 
 def parts_of(x, count):
     parts = []
-    for i in range(count):
+    for _ in range(count):
         part = x.astype(bf16).astype(f32)
         parts.append(part)
         x = x - part
@@ -66,7 +67,7 @@
 
 def sph_kernel(
     tile_dev, unroll, lists_ref, rim_lists_ref, own_ref, live_ref, below_ref, above_ref, density_ref, accel_ref,
-    feat_ref, featT_ref, own_feat_ref, coef_ref, coefb_ref, high_ref, low_ref, sum_ref, out_ref, q_ref,
+    partner_ref, mine_ref, turned_ref, weights_ref, coef_ref, coefb_ref, pair_ref, part_ref, out_ref,
 ):
     rows = own_ref.shape[-1]
     ext = tile_dev + 2 * RIM
@@ -88,57 +89,46 @@
     square = pos[0] * pos[0] + pos[1] * pos[1] + pos[2] * pos[2]
     log_mass = jnp.where(live, jnp.log2(jnp.where(live, mass, 1.0)), EMPTY_LOG)
     one, zero = jnp.ones_like(c), jnp.zeros_like(c)
-    partner_rows, own_rows = [], []
-    for value, own in [(pos[0], 2 * c * pos[0]), (pos[1], 2 * c * pos[1]), (pos[2], 2 * c * pos[2]), (square, -c)]:
-        p1, p2, p3 = parts_of(value, 3)
-        o1, o2, o3 = parts_of(own, 3)
-        partner_rows += [p1, p1, p2, p1, p3, p2]
-        own_rows += [o1, o2, o1, o3, o1, o2]
-    partner_rows += parts_of(log_mass, 3) + [one] * 3 + [zero] * 2
-    own_rows += [one] * 3 + parts_of(-c * square, 3) + [zero] * 2
-    for k in range(FEATURES):
-        feat_ref[:, k] = partner_rows[k]
+    for k, value in enumerate(pos + [square, log_mass, one, zero, zero]):
+        partner_ref[k * ext:(k + 1) * ext] = value
+    for k, value in enumerate([2 * c * x for x in pos] + [-c, one, -c * square, zero, zero]):
+        mine_ref[k * ext:(k + 1) * ext] = value
+    turn_fill = jnp.zeros((rows - DEPTH, rows), bf16)
 
     def turn(e):
-        block = feat_ref[e]
-        featT_ref[e] = jnp.concatenate([block, block], axis=0).T.astype(bf16)
-
-    pl.loop(0, ext, unroll=4)(turn)
-    for k in range(FEATURES):
-        feat_ref[:, k] = own_rows[k]
-    blank = jnp.zeros((FEATURES, rows), f32)
+        p1, p2, p3 = parts_of(partner_ref[pl.ds(e, 8, stride=ext)], 3)
+        block = jnp.concatenate([p1, p1, p2, p1, p3, p2], axis=0).astype(bf16)
+        turned_ref[e] = jnp.concatenate([block, turn_fill], axis=0).T
+
+    pl.loop(0, ext, unroll=8)(turn)
+    blank = jnp.zeros((rows, rows), bf16)
+
+    def own_weights(e):
+        o1, o2, o3 = parts_of(mine_ref[pl.ds(e, 8, stride=ext)], 3)
+        block = jnp.concatenate([o1, o2, o1, o3, o1, o2], axis=0).astype(bf16)
+        return jnp.concatenate([block, turn_fill], axis=0)
 
     def pair_up(p):
         e = HALO_TILES + 2 * p
-        a, b = feat_ref[e], feat_ref[e + 1]
-        top = jnp.concatenate([a, blank], axis=1)
-        low = jnp.concatenate([blank, b], axis=1)
-        own_feat_ref[p] = jnp.concatenate([top, low], axis=0).astype(bf16)
+        top = jnp.concatenate([own_weights(e), blank], axis=1)
+        low = jnp.concatenate([blank, own_weights(e + 1)], axis=1)
+        weights_ref[p] = jnp.concatenate([top, low], axis=0)
 
     pairs = (tile_dev + RIM) // 2
     pl.loop(0, pairs, unroll=4)(pair_up)
 
-    lane = lax.broadcasted_iota(jnp.int32, (rows, 2 * FEATURES), 1)
-    first_half = lane < FEATURES
-
-    def weights(p, partners):
-        own = own_feat_ref[p]
-        for e0, e1 in partners:
-            left = jnp.where(first_half, featT_ref[e0], featT_ref[e1])
-            yield jnp.exp2(dot(left, own))
-
     def density_pair(p, partners, store_at):
+        own = weights_ref[p]
         total = None
-        for n, t in enumerate(weights(p, partners)):
+        for n, (e0, e1) in enumerate(partners):
+            left = jnp.concatenate([turned_ref[e0], turned_ref[e1]], axis=1)
+            t = jnp.exp2(dot(left, own))
             if store_at is not None:
-                high = t.astype(bf16)
-                high_ref[store_at, n * rows:(n + 1) * rows] = high
-                low_ref[store_at, n * rows:(n + 1) * rows] = (t - high.astype(f32)).astype(bf16)
+                pair_ref[store_at, n * rows:(n + 1) * rows] = t
             part = jnp.sum(t.reshape(rows // 8, 8, 2 * rows), axis=0)
             total = part if total is None else total + part
-        total = jnp.sum(total, axis=0, keepdims=True)
-        sum_ref[pl.ds(2 * p, 1)] = total[:, :rows]
-        sum_ref[pl.ds(2 * p + 1, 1)] = total[:, rows:]
+        part_ref[pl.ds(16 * p, 8)] = total[:, :rows]
+        part_ref[pl.ds(16 * p + 8, 8)] = total[:, rows:]
 
     listed = lists_ref.shape[1]
 
@@ -159,20 +149,17 @@
         density_pair(u + rim_pairs, own_partners(u), u)
 
     inner = slice(HALO_TILES, ext - HALO_TILES)
-    raw = sum_ref[...] * norm[inner]
+    raw = sum(part_ref[pl.ds(k, tile_dev + RIM, stride=8)] for k in range(8))
+    raw = raw * norm[inner]
     inner_live = live[inner]
     q = jnp.where(inner_live, jnp.exp2(jnp.log2(jnp.where(inner_live, raw, 1.0)) * (-1.0 / 3.0)), 0.0)
     pad = jnp.zeros((HALO_TILES, rows), f32)
     q = jnp.concatenate([pad, q, pad], axis=0)
-    coef = [one]
-    for value in pos + [q] + [q * x for x in pos]:
-        coef += parts_of(value, 2)
-    coef.append(zero)
-    for k in range(SUMS):
-        coef_ref[:, k] = coef[k]
+    for k, value in enumerate([one] + pos + [q] + [q * x for x in pos]):
+        coef_ref[k * ext:(k + 1) * ext] = value
 
     def narrow(e):
-        coefb_ref[e] = coef_ref[e].astype(bf16)
+        coefb_ref[e] = jnp.concatenate(parts_of(coef_ref[pl.ds(e, 8, stride=ext)], 2), axis=0).astype(bf16)
 
     pl.loop(0, ext, unroll=8)(narrow)
 
@@ -181,23 +168,22 @@
         total = None
         for n, (e0, e1) in enumerate(own_partners(u)):
             left = jnp.concatenate([coefb_ref[e0], coefb_ref[e1]], axis=0)
-            part = dot(left, high_ref[u, n * rows:(n + 1) * rows]) + dot(left, low_ref[u, n * rows:(n + 1) * rows])
+            t = pair_ref[u, n * rows:(n + 1) * rows]
+            high = t.astype(bf16)
+            part = dot(left, high) + dot(left, (t - high.astype(f32)).astype(bf16))
             total = part if total is None else total + part
-        out_ref[2 * u] = total[:SUMS, :rows]
-        out_ref[2 * u + 1] = total[SUMS:, rows:]
+        out_ref[pl.ds(16 * u, 8)] = total[:8, :rows] + total[8:16, :rows]
+        out_ref[pl.ds(16 * u + 8, 8)] = total[16:24, rows:] + total[24:, rows:]
 
     mine = slice(RIM, RIM + tile_dev)
     own_live = live_ref[...]
     density_ref[...] = raw[HALO_TILES:HALO_TILES + tile_dev] * own_live
     q_own = q[mine]
     scale = own_live * (2.0 * inverse_sq[mine] * norm[mine])
-    s0 = out_ref[:, 0]
-    q0 = out_ref[:, 7] + out_ref[:, 8]
+    sums = [out_ref[pl.ds(k, tile_dev, stride=8)] for k in range(8)]
     for c in range(3):
-        s1 = out_ref[:, 1 + 2 * c] + out_ref[:, 2 + 2 * c]
-        q1 = out_ref[:, 9 + 2 * c] + out_ref[:, 10 + 2 * c]
         x = pos[c][mine]
-        accel_ref[c] = scale * (q_own * (x * s0 - s1) + (x * q0 - q1))
+        accel_ref[c] = scale * (q_own * (x * sums[0] - sums[1 + c]) + (x * sums[4] - sums[5 + c]))
 
 
 def sph(lists, rim_lists, own, live, below, above):
@@ -206,22 +192,22 @@
     listed = lists.shape[1]
     pairs = (tile_dev + RIM) // 2
     return pl.pallas_call(
-        functools.partial(sph_kernel, tile_dev, 4),
+        functools.partial(sph_kernel, tile_dev, 8),
         out_shape=(jax.ShapeDtypeStruct((tile_dev, rows), f32), jax.ShapeDtypeStruct((3, tile_dev, rows), f32)),
         in_specs=[SMEM, SMEM, VMEM, VMEM, VMEM, VMEM],
         out_specs=(VMEM, VMEM),
         scratch_shapes=[
-            pltpu.VMEM((ext, FEATURES, rows), f32),
-            pltpu.VMEM((ext, rows, 2 * FEATURES), bf16),
-            pltpu.VMEM((pairs, 2 * FEATURES, 2 * rows), bf16),
-            pltpu.VMEM((ext, SUMS, rows), f32),
-            pltpu.VMEM((ext, SUMS, rows), bf16),
-            pltpu.VMEM((tile_dev // 2, listed * rows, 2 * rows), bf16),
-            pltpu.VMEM((tile_dev // 2, listed * rows, 2 * rows), bf16),
-            pltpu.VMEM((tile_dev + RIM, rows), f32),
-            pltpu.VMEM((tile_dev, SUMS, rows), f32),
-            pltpu.VMEM((8, rows), f32),
+            pltpu.VMEM((8 * ext, rows), f32),
+            pltpu.VMEM((8 * ext, rows), f32),
+            pltpu.VMEM((ext, rows, rows), bf16),
+            pltpu.VMEM((pairs, 2 * rows, 2 * rows), bf16),
+            pltpu.VMEM((8 * ext, rows), f32),
+            pltpu.VMEM((ext, 16, rows), bf16),
+            pltpu.VMEM((tile_dev // 2, listed * rows, 2 * rows), f32),
+            pltpu.VMEM((8 * (tile_dev + RIM), rows), f32),
+            pltpu.VMEM((8 * tile_dev, rows), f32),
         ],
+        compiler_params=pltpu.CompilerParams(vmem_limit_bytes=40 << 20),
         name="sph",
     )(lists, rim_lists, own, live, below, above)
 

time: 41.1 us -> 37 us (0.900)
  Pallas kernels: 17.9 us -> 11.7 us
  local copies, waits for them, and re-layouts: 2.24 us -> 4.1 us
  waiting for transfers between devices: 9.67 us -> 10.3 us
  other arithmetic: 0.79 us -> 0.25 us
    pallas_call x1, Pallas kernels: 16 us -> 10.1 us  [sph(): pl.pallas_call(functools.partial(sph_kernel, tile_dev, 8), out_shape=(jax...]
    unnamed x13, local copies, waits for them, and re-layouts: 1.87 us -> 3.73 us
    all_to_all x1, waiting for transfers between devices: 3.17 us -> 3.78 us  [per_device(): own = lax.all_to_all(grouped, 'region', 0, 0, tiled=True)]
    convert_element_type x1, other arithmetic: 0.62 us -> 0.08 us  [per_device(): jnp.concatenate([below[FIELDS * RIM, :count], above[FIELDS * RIM, :count]])]
  transfers between devices with their start and end apart: 3 -> 3, of which waited for: 3 -> 3; matrix products, arithmetic and copies ran while one was open for 3% -> 2% of each run, Pallas kernels for 0% -> 0%
where the time goes in v2:
time: 37 us; the launch traced here: 36.6 us
  Pallas kernels  11.7 us (32%)
  waiting for transfers between devices  10.3 us (28%)
  starting transfers between devices  9.56 us (26%)
  local copies, waits for them, and re-layouts  4.1 us (11%)
  between operations  0.69 us (2%)
    pallas_call x1, Pallas kernels, sph(): pl.pallas_call(functools.partial(sph_kernel, tile_dev, 8), out_shape=(jax...  10.1 us
    ppermute x1, starting transfers between devices, per_device(): above = lax.ppermute(rim(True), 'sub', down)  5.11 us
    ppermute x1, waiting for transfers between devices, per_device(): below = lax.ppermute(rim(False), 'sub', up)  5.06 us
    all_to_all x1, starting transfers between devices, per_device(): own = lax.all_to_all(grouped, 'region', 0, 0, tiled=True)  4.4 us
    all_to_all x1, waiting for transfers between devices, per_device(): own = lax.all_to_all(grouped, 'region', 0, 0, tiled=True)  3.78 us
    unnamed x13, local copies, waits for them, and re-layouts  3.73 us
    pallas_call x1, Pallas kernels, group_tiles(): pl.pallas_call(functools.partial(group_kernel, per_dest), out_shape=jax.S...  1.52 us
    ppermute x1, waiting for transfers between devices, per_device(): above = lax.ppermute(rim(True), 'sub', down)  1.44 us
  transfers between devices with their start and end apart: 3, of which 3 were waited for; matrix products, arithmetic and copies ran while one was open for 2% of the time, Pallas kernels for 0%

profile of v2, /device:TPU:0, one launch (start us, length us, event | category | flops | bytes accessed | tf_op | source)
XLA Modules:
  0.0 36.6 jit_solution(8751825786969444433)
XLA Ops:
  0.6 0.0 copy-start
  0.6 0.9 %copy-done = f32[3,64,128]{2,1,0:T(8,128)S(1)} copy-done((f32[3,64,128]{2,1,0:T(8,128)S(1)}, f32[3,64,128]{2,1,0:T(8,128)}, u32[]{:S(2)}) %copy-start) | copy-done | bytes 98328
  1.5 0.0 copy-start.1
  1.5 0.8 %copy-done.1 = f32[64,128]{1,0:T(8,128)S(1)} copy-done((f32[64,128]{1,0:T(8,128)S(1)}, f32[64,128]{1,0:T(8,128)}, u32[]{:S(2)}) %copy-start.1) | copy-done | bytes 32792
  2.3 0.8 %copy-done.2 = f32[64,128]{1,0:T(8,128)S(1)} copy-done((f32[64,128]{1,0:T(8,128)S(1)}, f32[64,128]{1,0:T(8,128)}, u32[]{:S(2)}) %copy-start.2) | copy-done | bytes 32792
  3.0 0.7 %copy-done.3 = s32[64]{0:T(128)S(1)} copy-done((s32[64]{0:T(128)S(1)}, s32[64]{0:T(128)}, u32[]{:S(2)}) %copy-start.3) | copy-done | bytes 280
  3.7 1.5 %group_tiles.1 = f32[4,80,128]{2,1,0:T(8,128)} custom-call(s32[64]{0:T(128)S(1)} %copy-done.3, f32[3,64,128]{2,1,0:T(8,128)S(1)} %copy-done, f32[64,128]{1,0:T(8,128)S(1)} %copy-done.1, f32[64,128]{1,0:T(8,128)S(1)} %copy-done.2), custom_call_target="tpu_custom_call" | custom-call | tf_op jit(solution)/shard_map/group_tiles/pallas_call | solution.py:44
  5.2 4.4 %all-to-all-start = ((f32[4,80,128]{2,1,0:T(8,128)}), f32[4,80,128]{2,1,0:T(8,128)S(1)}, u32[]{:S(2)}, u32[]{:S(2)}) async-start(f32[4,80,128]{2,1,0:T(8,128)} %group_tiles.1), calls=%async_computation | async-start | bytes 327680 | tf_op jit(solution)/shard_map/all_to_all | solution.py:222
  9.6 0.0 copy-done.4
  9.6 0.1 slice_convert_fusion.1
  9.7 0.1 copy.10.lists_ref
  9.8 0.1 copy.8
  9.9 0.1 reshape.23
  10.0 0.1 copy.9
  10.1 0.1 reshape.25
  10.1 0.6 %copy-done.5 = s32[64]{0:T(128)S(1)} copy-done((s32[64]{0:T(128)S(1)}, s32[64]{0:T(128)}, u32[]{:S(2)}) %copy-start.5) | copy-done | bytes 280
  10.7 0.1 fusion.live_ref
  10.8 3.8 %all-to-all-done.own_ref = f32[4,80,128]{2,1,0:T(8,128)S(1)} async-done(((f32[4,80,128]{2,1,0:T(8,128)}), f32[4,80,128]{2,1,0:T(8,128)S(1)}, u32[]{:S(2)}, u32[]{:S(2)}) %all-to-all-start) | async-done | bytes 163872 | tf_op jit(solution)/shard_map/all_to_all | solution.py:222
  14.6 5.1 %collective-permute-start.1 = (f32[48,128]{1,0:T(8,128)S(1)}, f32[48,128]{1,0:T(8,128)S(1)}, u32[]{:S(2)}, u32[]{:S(2)}) collective-permute-start(f32[48,128]{1,0:T(8,128)S(1)} %select_maximum_fusion), channel_id=1, source_target_pairs={{1,0},{2,1},{3,2},{4,3},{5,4},{6,5},{7,6},{0,7},{9,8},{10,9},{11,1... | collective-permute-start | bytes 73736 | tf_op jit(solution)/shard_map/ppermute | solution.py:243
  19.8 0.1 collective-permute-start
  19.8 1.4 %collective-permute-done.1.above_ref = f32[48,128]{1,0:T(8,128)S(1)} collective-permute-done((f32[48,128]{1,0:T(8,128)S(1)}, f32[48,128]{1,0:T(8,128)S(1)}, u32[]{:S(2)}, u32[]{:S(2)}) %collective-permute-start.1) | collective-permute-done | bytes 24608 | tf_op jit(solution)/shard_map/ppermute | solution.py:243
  21.3 5.1 %collective-permute-done.below_ref = f32[48,128]{1,0:T(8,128)S(1)} collective-permute-done((f32[48,128]{1,0:T(8,128)S(1)}, f32[48,128]{1,0:T(8,128)S(1)}, u32[]{:S(2)}, u32[]{:S(2)}) %collective-permute-start) | collective-permute-done | bytes 24608 | tf_op jit(solution)/shard_map/ppermute | solution.py:242
  26.3 0.1 maximum_convert_fusion.rim_lists_ref
  26.4 10.1 %sph.1 = (f32[64,128]{1,0:T(8,128)}, f32[3,64,128]{2,1,0:T(8,128)}) custom-call(s32[64,4]{1,0:T(8,128)S(1)} %copy.10.lists_ref, s32[32]{0:T(128)S(1)} %maximum_convert_fusion.rim_lists_ref, f32[4,80,128]{2,1,0:T(8,128)S(1)} %all-to-all-done.own_ref, f32[64,128]{1,0:T(8,128)S(1)} %fusion.live_ref, f32[48,128]{1,0:T(8,128)S(1)} %collective-permute-done.below_ref, ...), custom_call_target="tpu_custom_call" | custom-call | tf_op jit(solution)/shard_map/sph/pallas_call | solution.py:194
  (14 shorter events, 0.1 us)
Async XLA Ops:
  0.6 0.9 %copy-start = (f32[3,64,128]{2,1,0:T(8,128)S(1)}, f32[3,64,128]{2,1,0:T(8,128)}, u32[]{:S(2)}) copy-start(f32[3,64,128]{2,1,0:T(8,128)} %coords_ref.1) | copy-start | bytes 294916
  1.5 0.8 %copy-start.1 = (f32[64,128]{1,0:T(8,128)S(1)}, f32[64,128]{1,0:T(8,128)}, u32[]{:S(2)}) copy-start(f32[64,128]{1,0:T(8,128)} %smooth_ref.1) | copy-start | bytes 98308
  2.3 0.8 %copy-start.2 = (f32[64,128]{1,0:T(8,128)S(1)}, f32[64,128]{1,0:T(8,128)}, u32[]{:S(2)}) copy-start(f32[64,128]{1,0:T(8,128)} %masses_ref.1) | copy-start | bytes 98308
  3.0 0.7 %copy-start.3 = (s32[64]{0:T(128)S(1)}, s32[64]{0:T(128)}, u32[]{:S(2)}) copy-start(s32[64]{0:T(128)} %owners_ref.1) | copy-start | bytes 772
  5.2 4.4 %copy-start.4 = (s32[64,4]{0,1:T(4,128)S(1)}, s32[64,4]{0,1:T(4,128)}, u32[]{:S(2)}) copy-start(s32[64,4]{0,1:T(4,128)} %param.11) | copy-start | bytes 3076
  5.2 9.3 %all-to-all-start = ((f32[4,80,128]{2,1,0:T(8,128)}), f32[4,80,128]{2,1,0:T(8,128)S(1)}, u32[]{:S(2)}, u32[]{:S(2)}) async-start(f32[4,80,128]{2,1,0:T(8,128)} %group_tiles.1), calls=%async_computation | async-start | bytes 327680 | tf_op jit(solution)/shard_map/all_to_all | solution.py:222
  10.1 0.7 %copy-start.5 = (s32[64]{0:T(128)S(1)}, s32[64]{0:T(128)}, u32[]{:S(2)}) copy-start(s32[64]{0:T(128)} %param.10) | copy-start | bytes 772
  14.6 6.6 %collective-permute-start.1 = (f32[48,128]{1,0:T(8,128)S(1)}, f32[48,128]{1,0:T(8,128)S(1)}, u32[]{:S(2)}, u32[]{:S(2)}) collective-permute-start(f32[48,128]{1,0:T(8,128)S(1)} %select_maximum_fusion), channel_id=1, source_target_pairs={{1,0},{2,1},{3,2},{4,3},{5,4},{6,5},{7,6},{0,7},{9,8},{10,9},{11,1... | collective-permute-start | bytes 73736 | tf_op jit(solution)/shard_map/ppermute | solution.py:243
  19.8 6.6 %collective-permute-start = (f32[48,128]{1,0:T(8,128)S(1)}, f32[48,128]{1,0:T(8,128)S(1)}, u32[]{:S(2)}, u32[]{:S(2)}) collective-permute-start(f32[48,128]{1,0:T(8,128)S(1)} %select_maximum_fusion.1), channel_id=1, source_target_pairs={{0,1},{1,2},{2,3},{3,4},{4,5},{5,6},{6,7},{7,0},{8,9},{9,10},{10,1... | collective-permute-start | bytes 73736 | tf_op jit(solution)/shard_map/ppermute | solution.py:242
